TPU v7x, 512 devices: a whole 4x4x16 slice. The times are simulated.
512 devices in a mesh: dp: 2 (over y_lo), tensor: 4 (over x), context: 64 (over z, y_hi, core).
Axes of the slice: x: 4, y: 4 (y_hi: 2, y_lo: 2; y = y_hi * 2 + y_lo), z: 16, core: 2. Of those that a mesh axis runs over, the one named last changes fastest.
Arguments:
- q_in: bfloat16 [2, 8192, 4096], P('dp', 'context', 'tensor'), may hold values from -44 to 44
- k_in: bfloat16 [2, 8192, 4096], P('dp', 'context', 'tensor'), may hold values from -6 to 6
- v_in: bfloat16 [2, 8192, 4096], P('dp', 'context', 'tensor'), may hold values from -6 to 6
- short_filt: float32 [3, 7, 4096], P(None, None, 'tensor'), may hold values from -2 to 2
- long_filt: float32 [8192, 4096], P('context', 'tensor'), may hold values from -1.1 to 1.1
- norm_gain: float32 [4096], P('tensor'), may hold values from 0.1 to 1.9
- grad_out: bfloat16 [2, 8192, 4096], P('dp', 'context', 'tensor'), may hold values from -6 to 6
Outputs:
- mixed: bfloat16 [2, 8192, 4096], P('dp', 'context', 'tensor')
- grad_inputs: bfloat16 [3, 2, 8192, 4096], P(None, 'dp', 'context', 'tensor')
- grad_long: float32 [8192, 4096], P('context', 'tensor')
- grad_short: float32 [3, 7, 4096], P(None, None, 'tensor')
All inputs are finite; a program needn't handle non-finite values.
Results may differ from a plain program's by a relative error of at most 0.00225.
Values may be sent and summed in bfloat16 or wider, within the bound.
No kernel may reach another device: no remote copies, remote signals or barrier semaphores. Data moves between devices by JAX's collectives and lax.ppermute only.
A program may use at most 128 MiB of HBM per device.

v0:
```python
import math
import jax
import jax.numpy as jnp
from jax import lax
from jax.sharding import PartitionSpec as P

D = 4096
FILT = 7
EPS = 1e-06
HIGH = lax.Precision.HIGHEST


def passed_along(shard, axis, by):
    peers = lax.axis_size(axis)
    pairs = [(i, i + by) for i in range(peers) if 0 <= i + by < peers]
    return lax.ppermute(shard, axis, pairs)


def phases(first, second, modulus):
    product = first[:, None] * second[None, :] % modulus
    return product.astype(jnp.float32) * (2.0 * math.pi / modulus)


def block_table(block_len, sign):
    index = jnp.arange(block_len, dtype=jnp.int32)
    angle = phases(index, index, block_len)
    cosine = jnp.cos(angle)
    sine = jnp.sin(angle) * sign
    return jnp.stack([jnp.stack([cosine, sine]), jnp.stack([-sine, cosine])])


def forward_rows(values, modulus):
    count, block_len, width = values.shape
    ctx_size = lax.axis_size("context")
    sub_len = block_len // ctx_size
    spread = lax.all_to_all(
        values.reshape(count, 1, block_len, width),
        "context",
        split_axis=2,
        concat_axis=1,
        tiled=True,
    )
    freq = jnp.arange(2 * ctx_size, dtype=jnp.int32)
    place = (
        jnp.arange(ctx_size, dtype=jnp.int32)[:, None] * block_len
        + lax.axis_index("context") * sub_len
        + jnp.arange(sub_len, dtype=jnp.int32)[None, :]
    )
    angle = (freq[:, None, None] * place[None] % modulus).astype(jnp.float32) * (
        2.0 * math.pi / modulus
    )
    table = jnp.stack([jnp.cos(angle), -jnp.sin(angle)])
    turned = jnp.einsum("pkcs,ncsx->npksx", table, spread, precision=HIGH)
    moved = lax.all_to_all(turned, "context", split_axis=2, concat_axis=3, tiled=True)
    return jnp.einsum("pqmb,nqjbx->npjmx", block_table(block_len, 1.0), moved, precision=HIGH)


def inverse_rows(spec, modulus):
    rows = spec.shape[2]
    block_len = spec.shape[3]
    ctx_size = lax.axis_size("context")
    index = jnp.arange(block_len, dtype=jnp.int32)
    freq = 2 * lax.axis_index("context") + jnp.arange(rows, dtype=jnp.int32)
    total = freq[:, None, None] + 2 * ctx_size * index[None, :, None]
    angle = (total * index[None, None, :] % modulus).astype(jnp.float32) * (2.0 * math.pi / modulus)
    cosine = jnp.cos(angle)
    sine = jnp.sin(angle)
    table = jnp.stack([jnp.stack([cosine, -sine]), jnp.stack([sine, cosine])])
    turned = jnp.einsum("pqjmb,nqjmx->npjbx", table, spec, precision=HIGH)
    moved = lax.all_to_all(turned, "context", split_axis=3, concat_axis=2, tiled=True)
    outer = phases(
        jnp.arange(ctx_size, dtype=jnp.int32),
        jnp.arange(2 * ctx_size, dtype=jnp.int32),
        2 * ctx_size,
    )
    real_table = jnp.stack([jnp.cos(outer), -jnp.sin(outer)])
    values = jnp.einsum("qck,nqksx->ncsx", real_table, moved, precision=HIGH) / modulus
    back = lax.all_to_all(values, "context", split_axis=1, concat_axis=2, tiled=True)
    return back.reshape(back.shape[0], back.shape[2], back.shape[3])


def shards(q_in, k_in, v_in, short_filt, long_filt, norm_gain, grad_out):
    block_len = q_in.shape[1]
    channels = q_in.shape[2]
    edge_rows = FILT - 1
    modulus = 2 * lax.axis_size("context") * block_len
    branches = jnp.stack([q_in[0], k_in[0], v_in[0]])
    before = passed_along(branches[:, block_len - edge_rows :], "context", 1)
    inputs = jnp.concatenate([before, branches], 1).astype(jnp.float32)
    shorts = jnp.zeros((3, block_len, channels), jnp.float32)
    for lag in range(FILT):
        shorts = (
            shorts
            + short_filt[:, lag][:, None, :]
            * inputs[:, edge_rows - lag : edge_rows - lag + block_len]
        )
    q_short = shorts[0]
    k_short = shorts[1]
    v_short = shorts[2]
    kv_prod = k_short * v_short
    spectra = forward_rows(jnp.stack([kv_prod, long_filt]), modulus)
    kv_real, kv_imag = (spectra[0, 0], spectra[0, 1])
    filt_real, filt_imag = (spectra[1, 0], spectra[1, 1])
    conv_spec = jnp.stack(
        [kv_real * filt_real - kv_imag * filt_imag, kv_real * filt_imag + kv_imag * filt_real]
    )[None]
    conv = inverse_rows(conv_spec, modulus)[0]
    y_out = q_short * conv
    squares = lax.psum(jnp.sum(y_out * y_out, axis=-1), "tensor")
    rms = jnp.sqrt(squares / D + EPS)[:, None]
    mixed = (y_out / rms * norm_gain).astype(jnp.bfloat16)[None]
    grad_z = grad_out[0].astype(jnp.float32) * norm_gain
    prods = lax.psum(jnp.sum(grad_z * y_out, axis=-1), "tensor")[:, None]
    grad_y = grad_z / rms - y_out * prods / (D * rms**3)
    dconv = grad_y * q_short
    grad_q = grad_y * conv
    grad_spec = forward_rows(dconv[None], modulus)[0]
    grad_real = grad_spec[0]
    grad_imag = grad_spec[1]
    dkv_spec = jnp.stack(
        [
            filt_real * grad_real + filt_imag * grad_imag,
            filt_real * grad_imag - filt_imag * grad_real,
        ]
    )
    dfilt_spec = jnp.stack(
        [kv_real * grad_real + kv_imag * grad_imag, kv_real * grad_imag - kv_imag * grad_real]
    )
    results = inverse_rows(jnp.stack([dkv_spec, dfilt_spec]), modulus)
    dkv = results[0]
    dfilt_local = results[1]
    grads = jnp.stack([grad_q, dkv * v_short, dkv * k_short])
    after = passed_along(grads[:, :edge_rows].astype(jnp.bfloat16), "context", -1).astype(
        jnp.float32
    )
    extended = jnp.concatenate([grads, after], 1)
    grad_inputs = jnp.zeros((3, block_len, channels), jnp.float32)
    for lag in range(FILT):
        grad_inputs = (
            grad_inputs + short_filt[:, lag][:, None, :] * extended[:, lag : lag + block_len]
        )
    short_local = jnp.stack(
        [
            jnp.sum(grads * inputs[:, edge_rows - lag : edge_rows - lag + block_len], axis=1)
            for lag in range(FILT)
        ],
        1,
    )
    scale = 1.0 / math.sqrt(lax.axis_size("dp") * block_len * lax.axis_size("context"))
    grad_long = lax.psum(dfilt_local, "dp") * scale
    grad_short = lax.psum(short_local, ("dp", "context")) * scale
    return (mixed, grad_inputs.astype(jnp.bfloat16)[:, None], grad_long, grad_short)


def solution(mesh):
    in_specs = (
        P("dp", "context", "tensor"),
        P("dp", "context", "tensor"),
        P("dp", "context", "tensor"),
        P(None, None, "tensor"),
        P("context", "tensor"),
        P("tensor"),
        P("dp", "context", "tensor"),
    )
    out_specs = (
        P("dp", "context", "tensor"),
        P(None, "dp", "context", "tensor"),
        P("context", "tensor"),
        P(None, None, "tensor"),
    )
    return jax.shard_map(shards, mesh=mesh, in_specs=in_specs, out_specs=out_specs, check_vma=False)
```

profile of v0, /device:TPU:1, one launch (start us, length us, event | category | flops | bytes accessed | tf_op | source)
XLA Modules:
  0.0 1352.6 jit_solution(16455876887592393104)
XLA Ops:
  11.4 6.2 collective-permute-start
  31.3 17.8 %all-to-all-start = ((f32[2,1,128,1024]{3,0,1,2:T(2,128)}), f32[2,1,128,1024]{3,0,1,2:T(2,128)S(1)}, u32[]{:S(2)}, u32[]{:S(2)}) async-start(f32[2,1,128,1024]{3,0,1,2:T(2,128)} %maximum_bitcast_fusion.4), calls=%async_computation | async-start | bytes 2097152 | tf_op jit(solution)/shard_map/all_to_all | solution.py:36
  49.5 53.7 %all-to-all-done = f32[2,1,128,1024]{3,0,1,2:T(2,128)S(1)} async-done(((f32[2,1,128,1024]{3,0,1,2:T(2,128)}), f32[2,1,128,1024]{3,0,1,2:T(2,128)S(1)}, u32[]{:S(2)}, u32[]{:S(2)}) %all-to-all-start) | async-done | bytes 1048608 | tf_op jit(solution)/shard_map/all_to_all | solution.py:36
  108.3 7.3 copy.68
  115.6 7.8 all-to-all-start.1
  124.8 184.3 %all-to-all-done.1 = f32[2,2,128,2,1024]{4,1,0,3,2:T(2,128)} async-done(((f32[2,2,128,2,1024]{4,1,0,3,2:T(2,128)}), f32[2,2,128,2,1024]{4,1,0,3,2:T(2,128)}, u32[]{:S(2)}, u32[]{:S(2)}) %all-to-all-start.1) | async-done | bytes 4194336 | tf_op jit(solution)/shard_map/all_to_all | solution.py:54
  309.1 5.4 copy.70
  314.5 8.1 fusion.4
  332.2 10.6 all-to-all-start.2
  343.0 98.5 %all-to-all-done.2 = f32[1,2,2,128,1024]{4,1,2,0,3:T(2,128)} async-done(((f32[1,2,2,128,1024]{4,1,2,0,3:T(2,128)}), f32[1,2,2,128,1024]{4,1,2,0,3:T(2,128)}, u32[]{:S(2)}, u32[]{:S(2)}) %all-to-all-start.2) | async-done | bytes 2097184 | tf_op jit(solution)/shard_map/all_to_all | solution.py:70
  454.3 7.7 all-to-all-start.3
  463.2 32.8 %all-to-all-done.3 = f32[1,64,2,1024]{3,2,0,1:T(2,128)S(1)} async-done(((f32[1,64,2,1024]{3,2,0,1:T(2,128)}), f32[1,64,2,1024]{3,2,0,1:T(2,128)S(1)}, u32[]{:S(2)}, u32[]{:S(2)}) %all-to-all-start.3) | async-done | bytes 524320 | tf_op jit(solution)/shard_map/all_to_all | solution.py:78
  499.4 9.3 all-reduce
  514.5 40.9 %all_to_all.105 = f32[1,1,128,1024]{3,0,1,2:T(1,128)} all-to-all(f32[1,1,128,1024]{3,0,1,2:T(1,128)S(1)} %fusion.48), channel_id=1, replica_groups=mesh['dp'=2,'tensor'=4,'context'=64] {'context'}, dimensions={2} | all-to-all | bytes 1048576 | tf_op jit(solution)/shard_map/all_to_all | solution.py:36
  569.1 103.5 %all_to_all.106 = f32[1,2,128,2,1024]{4,1,3,0,2:T(2,128)S(1)} all-to-all(f32[1,2,128,2,1024]{4,1,3,0,2:T(2,128)} %copy.86), channel_id=1, replica_groups=mesh['dp'=2,'tensor'=4,'context'=64] {'context'}, dimensions={2} | all-to-all | bytes 4194304 | tf_op jit(solution)/shard_map/all_to_all | solution.py:54
  689.7 7.3 copy.95
  697.1 196.5 %all_to_all.107 = f32[2,2,2,128,1024]{4,1,0,2,3:T(2,128)S(1)} all-to-all(f32[2,2,2,128,1024]{4,1,0,2,3:T(2,128)} %copy.95), channel_id=1, replica_groups=mesh['dp'=2,'tensor'=4,'context'=64] {'context'}, dimensions={3} | all-to-all | bytes 8388608 | tf_op jit(solution)/shard_map/all_to_all | solution.py:70
  893.6 5.3 copy.97
  898.8 6.0 all_to_all.95
  911.2 8.2 all-to-all-start.7
  921.1 52.3 %all-to-all-done.7 = f32[2,64,2,1024]{3,2,0,1:T(2,128)} async-done(((f32[2,64,2,1024]{3,2,0,1:T(2,128)}), f32[2,64,2,1024]{3,2,0,1:T(2,128)}, u32[]{:S(2)}, u32[]{:S(2)}) %all-to-all-start.7) | async-done | bytes 1048608 | tf_op jit(solution)/shard_map/all_to_all | solution.py:78
  977.1 7.5 fusion.41
  1009.0 289.3 %all-reduce.6.cloned.1.call-done = f32[3,7,1024]{2,0,1:T(4,128)} async-done(((f32[3,7,1024]{2,0,1:T(4,128)}), f32[3,7,1024]{2,0,1:T(4,128)}) %all-reduce.6.cloned.1.call-update) | async-done | bytes 86032 | tf_op jit(solution)/shard_map/psum | solution.py:151
  1299.9 43.4 %all-reduce.4.cloned.1.call-done = f32[128,1024]{1,0:T(8,128)} async-done(((f32[128,1024]{1,0:T(8,128)}), f32[128,1024]{1,0:T(8,128)}) %all-reduce.4.cloned.1.call-update) | async-done | bytes 524304 | tf_op jit(solution)/shard_map/psum | solution.py:150
  (151 shorter events, 127.6 us)
Async XLA Ops:
  7.2 10.5 copy-start.28
  7.2 10.7 copy-start.12
  11.4 8.9 collective-permute-start
  31.3 71.9 %all-to-all-start = ((f32[2,1,128,1024]{3,0,1,2:T(2,128)}), f32[2,1,128,1024]{3,0,1,2:T(2,128)S(1)}, u32[]{:S(2)}, u32[]{:S(2)}) async-start(f32[2,1,128,1024]{3,0,1,2:T(2,128)} %maximum_bitcast_fusion.4), calls=%async_computation | async-start | bytes 2097152 | tf_op jit(solution)/shard_map/all_to_all | solution.py:36
  49.4 58.9 %copy-start.10 = (f32[1,128,64,2]{1,2,0,3:T(8,128)}, f32[1,128,64,2]{1,2,0,3:T(8,128)S(1)}, u32[]{:S(2)}) copy-start(f32[1,128,64,2]{1,2,0,3:T(8,128)S(1)} %get-tuple-element.55) | copy-start | bytes 196612
  49.5 58.9 %copy-start.11 = (f32[1,128,64,2]{1,2,0,3:T(8,128)}, f32[1,128,64,2]{1,2,0,3:T(8,128)S(1)}, u32[]{:S(2)}) copy-start(f32[1,128,64,2]{1,2,0,3:T(8,128)S(1)} %get-tuple-element.56) | copy-start | bytes 196612
  115.6 193.4 %all-to-all-start.1 = ((f32[2,2,128,2,1024]{4,1,0,3,2:T(2,128)}), f32[2,2,128,2,1024]{4,1,0,3,2:T(2,128)}, u32[]{:S(2)}, u32[]{:S(2)}) async-start(f32[2,2,128,2,1024]{4,1,0,3,2:T(2,128)} %copy.68), calls=%async_computation.1 | async-start | bytes 8388608 | tf_op jit(solution)/shard_map/all_to_all | solution.py:54
  124.0 190.5 %copy-start.8 = (f32[1,2,128,128]{3,2,1,0:T(8,128)}, f32[1,2,128,128]{3,2,1,0:T(8,128)S(1)}, u32[]{:S(2)}) copy-start(f32[1,2,128,128]{3,2,1,0:T(8,128)S(1)} %get-tuple-element.50) | copy-start | bytes 393220
  124.0 190.5 %copy-start.9 = (f32[1,2,128,128]{3,2,1,0:T(8,128)}, f32[1,2,128,128]{3,2,1,0:T(8,128)S(1)}, u32[]{:S(2)}) copy-start(f32[1,2,128,128]{3,2,1,0:T(8,128)S(1)} %get-tuple-element.51) | copy-start | bytes 393220
  332.2 109.2 %all-to-all-start.2 = ((f32[1,2,2,128,1024]{4,1,2,0,3:T(2,128)}), f32[1,2,2,128,1024]{4,1,2,0,3:T(2,128)}, u32[]{:S(2)}, u32[]{:S(2)}) async-start(f32[1,2,2,128,1024]{4,1,2,0,3:T(2,128)} %copy.79), calls=%async_computation.2 | async-start | bytes 4194304 | tf_op jit(solution)/shard_map/all_to_all | solution.py:70
  342.9 107.1 %copy-start.13 = (f32[1,64,128]{2,1,0:T(8,128)}, f32[1,64,128]{2,1,0:T(8,128)S(1)}, u32[]{:S(2)}) copy-start(f32[1,64,128]{2,1,0:T(8,128)S(1)} %get-tuple-element.68) | copy-start | bytes 98308
  450.0 12.0 copy-start.5
  454.3 41.7 %all-to-all-start.3 = ((f32[1,64,2,1024]{3,2,0,1:T(2,128)}), f32[1,64,2,1024]{3,2,0,1:T(2,128)S(1)}, u32[]{:S(2)}, u32[]{:S(2)}) async-start(f32[1,64,2,1024]{3,2,0,1:T(2,128)} %copy.82), calls=%async_computation.3 | async-start | bytes 1048576 | tf_op jit(solution)/shard_map/all_to_all | solution.py:78
  898.8 6.0 copy-start.14
  911.2 62.2 %all-to-all-start.7 = ((f32[2,64,2,1024]{3,2,0,1:T(2,128)}), f32[2,64,2,1024]{3,2,0,1:T(2,128)}, u32[]{:S(2)}, u32[]{:S(2)}) async-start(f32[2,64,2,1024]{3,2,0,1:T(2,128)} %copy.98), calls=%async_computation.7 | async-start | bytes 2097152 | tf_op jit(solution)/shard_map/all_to_all | solution.py:78
  919.5 57.7 %copy-start.29 = (f32[1024]{0:T(1024)S(1)}, f32[1024]{0:T(1024)}, u32[]{:S(2)}) copy-start(f32[1024]{0:T(1024)} %param.12) | copy-start | bytes 12292
  919.5 57.6 %copy-start.30 = (f32[128]{0:T(128)S(1)}, f32[128]{0:T(128)}, u32[]{:S(2)}) copy-start(f32[128]{0:T(128)} %get-tuple-element.22) | copy-start | bytes 1540
  919.5 57.6 %copy-start.31 = (f32[128]{0:T(128)S(1)}, f32[128]{0:T(128)}, u32[]{:S(2)}) copy-start(f32[128]{0:T(128)} %get-tuple-element.57) | copy-start | bytes 1540
  919.5 57.6 %copy-start.32 = (f32[128]{0:T(128)S(1)}, f32[128]{0:T(128)}, u32[]{:S(2)}) copy-start(f32[128]{0:T(128)} %get-tuple-element.58) | copy-start | bytes 1540
  919.5 378.8 %all-reduce.6.cloned.1.call-start = ((), (), s32[]{:S(2)}) async-start(), calls=%async_computation.9 | async-start | bytes 229376 | tf_op jit(solution)/shard_map/psum | solution.py:151
  989.0 8.1 copy-start.7
  989.0 9.3 copy-start.6
  989.8 353.6 %all-reduce.4.cloned.1.call-start = ((), (), s32[]{:S(2)}) async-start(), calls=%async_computation.8 | async-start | bytes 1048576 | tf_op jit(solution)/shard_map/psum | solution.py:150
  992.6 8.8 collective-permute-start.1
  (18 other events, 72.9 us)
Sparse Core Ops, SparseCore 0:
  989.9 308.3 all-reduce.5
  1301.2 42.1 all-reduce.3
where the time goes:
time: 1360 us; the launch traced here: 1350 us
  waiting for transfers between devices  759 us (56%)
  blocking collectives  350 us (26%)
  local copies, waits for them, and re-layouts  81.6 us (6%)
  starting transfers between devices  63.1 us (5%)
  other arithmetic  46.6 us (3%)
  matrix products  37.2 us (3%)
  between operations  15.3 us (1%)
    psum x1, waiting for transfers between devices, shards(): grad_short = lax.psum(short_local, ('dp', 'context')) * scale  289 us
    all_to_all x1, blocking collectives, inverse_rows(): lax.all_to_all(turned, 'context', split_axis=3, concat_axis=2, tiled=True)  196 us
    all_to_all x1, waiting for transfers between devices, forward_rows(): lax.all_to_all(turned, 'context', split_axis=2, concat_axis=3, tiled=True)  184 us
    all_to_all x1, blocking collectives, forward_rows(): lax.all_to_all(turned, 'context', split_axis=2, concat_axis=3, tiled=True)  103 us
    all_to_all x1, waiting for transfers between devices, inverse_rows(): lax.all_to_all(turned, 'context', split_axis=3, concat_axis=2, tiled=True)  98.5 us
    all_to_all x2, waiting for transfers between devices, inverse_rows(): lax.all_to_all(values, 'context', split_axis=1, concat_axis=2, tiled=True)  85 us
    all_to_all x1, waiting for transfers between devices, forward_rows(): lax.all_to_all(values.reshape(count, 1, block_len, width), 'context', spl...  53.7 us
    psum x1, waiting for transfers between devices, shards(): grad_long = lax.psum(dfilt_local, 'dp') * scale  43.4 us
  transfers between devices with their start and end apart: 9, of which 9 were waited for; matrix products, arithmetic and copies ran while one was open for 1% of the time, Pallas kernels for 0%

commit v1 on v0

--- a/solution.py
+++ b/solution.py
@@ -148,7 +148,7 @@
     )
     scale = 1.0 / math.sqrt(lax.axis_size("dp") * block_len * lax.axis_size("context"))
     grad_long = lax.psum(dfilt_local, "dp") * scale
-    grad_short = lax.psum(short_local, ("dp", "context")) * scale
+    grad_short = jnp.sum(lax.all_gather(short_local, ("dp", "context")), 0) * scale
     return (mixed, grad_inputs.astype(jnp.bfloat16)[:, None], grad_long, grad_short)
 
 

time: 1360 us -> 1240 us (0.912)
  waiting for transfers between devices: 759 us -> 632 us
    psum x1 -> x0, waiting for transfers between devices: 289 us -> none  [shards(): grad_short = lax.psum(short_local, ('dp', 'context')) * scale]
    all_gather x0 -> x1, waiting for transfers between devices: none -> 195 us  [shards(): lax.all_gather(short_local, ('dp', 'context'))]
    psum x1, waiting for transfers between devices: 43.4 us -> 9.67 us  [shards(): grad_long = lax.psum(dfilt_local, 'dp') * scale]
  transfers between devices with their start and end apart: 9 -> 9, of which waited for: 9 -> 9; matrix products, arithmetic and copies ran while one was open for 1% -> 3% of each run, Pallas kernels for 0% -> 0%
where the time goes in v1:
time: 1240 us; the launch traced here: 1230 us
  waiting for transfers between devices  632 us (51%)
  blocking collectives  350 us (28%)
  local copies, waits for them, and re-layouts  80.3 us (6%)
  starting transfers between devices  62.8 us (5%)
  other arithmetic  51.3 us (4%)
  matrix products  37.2 us (3%)
  between operations  16.7 us (1%)
    all_to_all x1, blocking collectives, inverse_rows(): lax.all_to_all(turned, 'context', split_axis=3, concat_axis=2, tiled=True)  196 us
    all_gather x1, waiting for transfers between devices, shards(): lax.all_gather(short_local, ('dp', 'context'))  195 us
    all_to_all x1, waiting for transfers between devices, forward_rows(): lax.all_to_all(turned, 'context', split_axis=2, concat_axis=3, tiled=True)  184 us
    all_to_all x1, blocking collectives, forward_rows(): lax.all_to_all(turned, 'context', split_axis=2, concat_axis=3, tiled=True)  103 us
    all_to_all x1, waiting for transfers between devices, inverse_rows(): lax.all_to_all(turned, 'context', split_axis=3, concat_axis=2, tiled=True)  98.5 us
    all_to_all x2, waiting for transfers between devices, inverse_rows(): lax.all_to_all(values, 'context', split_axis=1, concat_axis=2, tiled=True)  85.1 us
    all_to_all x1, waiting for transfers between devices, forward_rows(): lax.all_to_all(values.reshape(count, 1, block_len, width), 'context', spl...  53.7 us
    all_to_all x1, blocking collectives, forward_rows(): lax.all_to_all(values.reshape(count, 1, block_len, width), 'context', spl...  40.9 us
  transfers between devices with their start and end apart: 9, of which 9 were waited for; matrix products, arithmetic and copies ran while one was open for 3% of the time, Pallas kernels for 0%

profile of v1, /device:TPU:1, one launch (start us, length us, event | category | flops | bytes accessed | tf_op | source)
XLA Modules:
  0.0 1230.6 jit_solution(9815066965378334629)
XLA Ops:
  12.3 6.2 collective-permute-start
  32.1 17.8 %all-to-all-start = ((f32[2,1,128,1024]{3,0,1,2:T(2,128)}), f32[2,1,128,1024]{3,0,1,2:T(2,128)S(1)}, u32[]{:S(2)}, u32[]{:S(2)}) async-start(f32[2,1,128,1024]{3,0,1,2:T(2,128)} %maximum_bitcast_fusion.4), calls=%async_computation | async-start | bytes 2097152 | tf_op jit(solution)/shard_map/all_to_all | solution.py:36
  50.3 53.7 %all-to-all-done = f32[2,1,128,1024]{3,0,1,2:T(2,128)S(1)} async-done(((f32[2,1,128,1024]{3,0,1,2:T(2,128)}), f32[2,1,128,1024]{3,0,1,2:T(2,128)S(1)}, u32[]{:S(2)}, u32[]{:S(2)}) %all-to-all-start) | async-done | bytes 1048608 | tf_op jit(solution)/shard_map/all_to_all | solution.py:36
  109.2 7.3 copy.67
  116.5 7.8 all-to-all-start.1
  125.6 184.3 %all-to-all-done.1 = f32[2,2,128,2,1024]{4,1,0,3,2:T(2,128)} async-done(((f32[2,2,128,2,1024]{4,1,0,3,2:T(2,128)}), f32[2,2,128,2,1024]{4,1,0,3,2:T(2,128)}, u32[]{:S(2)}, u32[]{:S(2)}) %all-to-all-start.1) | async-done | bytes 4194336 | tf_op jit(solution)/shard_map/all_to_all | solution.py:54
  309.9 5.4 copy.69
  315.4 8.1 fusion.4
  333.0 10.6 all-to-all-start.2
  343.8 98.5 %all-to-all-done.2 = f32[1,2,2,128,1024]{4,1,2,0,3:T(2,128)} async-done(((f32[1,2,2,128,1024]{4,1,2,0,3:T(2,128)}), f32[1,2,2,128,1024]{4,1,2,0,3:T(2,128)}, u32[]{:S(2)}, u32[]{:S(2)}) %all-to-all-start.2) | async-done | bytes 2097184 | tf_op jit(solution)/shard_map/all_to_all | solution.py:70
  455.2 7.6 all-to-all-start.3
  464.0 32.8 %all-to-all-done.3 = f32[1,64,2,1024]{3,2,0,1:T(2,128)S(1)} async-done(((f32[1,64,2,1024]{3,2,0,1:T(2,128)}), f32[1,64,2,1024]{3,2,0,1:T(2,128)S(1)}, u32[]{:S(2)}, u32[]{:S(2)}) %all-to-all-start.3) | async-done | bytes 524320 | tf_op jit(solution)/shard_map/all_to_all | solution.py:78
  500.1 9.3 all-reduce
  515.3 40.9 %all_to_all.105 = f32[1,1,128,1024]{3,0,1,2:T(1,128)} all-to-all(f32[1,1,128,1024]{3,0,1,2:T(1,128)S(1)} %fusion.48), channel_id=1, replica_groups=mesh['dp'=2,'tensor'=4,'context'=64] {'context'}, dimensions={2} | all-to-all | bytes 1048576 | tf_op jit(solution)/shard_map/all_to_all | solution.py:36
  569.9 103.5 %all_to_all.106 = f32[1,2,128,2,1024]{4,1,3,0,2:T(2,128)S(1)} all-to-all(f32[1,2,128,2,1024]{4,1,3,0,2:T(2,128)} %copy.85), channel_id=1, replica_groups=mesh['dp'=2,'tensor'=4,'context'=64] {'context'}, dimensions={2} | all-to-all | bytes 4194304 | tf_op jit(solution)/shard_map/all_to_all | solution.py:54
  690.5 7.3 copy.94
  697.8 196.5 %all_to_all.107 = f32[2,2,2,128,1024]{4,1,0,2,3:T(2,128)S(1)} all-to-all(f32[2,2,2,128,1024]{4,1,0,2,3:T(2,128)} %copy.94), channel_id=1, replica_groups=mesh['dp'=2,'tensor'=4,'context'=64] {'context'}, dimensions={3} | all-to-all | bytes 8388608 | tf_op jit(solution)/shard_map/all_to_all | solution.py:70
  899.6 6.0 all_to_all.95
  912.0 8.2 all-to-all-start.7
  921.9 52.3 %all-to-all-done.7 = f32[2,64,2,1024]{3,2,0,1:T(2,128)} async-done(((f32[2,64,2,1024]{3,2,0,1:T(2,128)}), f32[2,64,2,1024]{3,2,0,1:T(2,128)}, u32[]{:S(2)}, u32[]{:S(2)}) %all-to-all-start.7) | async-done | bytes 1048608 | tf_op jit(solution)/shard_map/all_to_all | solution.py:78
  978.3 7.8 fusion.41
  1009.5 9.7 all-reduce.3.cloned.1.call-done
  1021.1 195.2 %all-gather.3.cloned.1.call-done = f32[384,7,1024]{2,1,0:T(8,128)} async-done(((f32[3,7,1024]{2,1,0:T(8,128)}), f32[384,7,1024]{2,1,0:T(8,128)}) %all-gather.3.cloned.1.call-update) | async-done | bytes 11010064 | tf_op jit(solution)/shard_map/all_gather | solution.py:151
  1216.2 5.8 reduce_sum.99
  (148 shorter events, 131.3 us)
Async XLA Ops:
  8.0 10.5 copy-start.26
  8.0 10.7 copy-start.11
  12.3 8.9 collective-permute-start
  32.1 71.9 %all-to-all-start = ((f32[2,1,128,1024]{3,0,1,2:T(2,128)}), f32[2,1,128,1024]{3,0,1,2:T(2,128)S(1)}, u32[]{:S(2)}, u32[]{:S(2)}) async-start(f32[2,1,128,1024]{3,0,1,2:T(2,128)} %maximum_bitcast_fusion.4), calls=%async_computation | async-start | bytes 2097152 | tf_op jit(solution)/shard_map/all_to_all | solution.py:36
  50.3 58.9 %copy-start.9 = (f32[1,128,64,2]{1,2,0,3:T(8,128)}, f32[1,128,64,2]{1,2,0,3:T(8,128)S(1)}, u32[]{:S(2)}) copy-start(f32[1,128,64,2]{1,2,0,3:T(8,128)S(1)} %get-tuple-element.55) | copy-start | bytes 196612
  50.3 58.9 %copy-start.10 = (f32[1,128,64,2]{1,2,0,3:T(8,128)}, f32[1,128,64,2]{1,2,0,3:T(8,128)S(1)}, u32[]{:S(2)}) copy-start(f32[1,128,64,2]{1,2,0,3:T(8,128)S(1)} %get-tuple-element.56) | copy-start | bytes 196612
  116.5 193.4 %all-to-all-start.1 = ((f32[2,2,128,2,1024]{4,1,0,3,2:T(2,128)}), f32[2,2,128,2,1024]{4,1,0,3,2:T(2,128)}, u32[]{:S(2)}, u32[]{:S(2)}) async-start(f32[2,2,128,2,1024]{4,1,0,3,2:T(2,128)} %copy.67), calls=%async_computation.1 | async-start | bytes 8388608 | tf_op jit(solution)/shard_map/all_to_all | solution.py:54
  124.9 190.5 %copy-start.7 = (f32[1,2,128,128]{3,2,1,0:T(8,128)}, f32[1,2,128,128]{3,2,1,0:T(8,128)S(1)}, u32[]{:S(2)}) copy-start(f32[1,2,128,128]{3,2,1,0:T(8,128)S(1)} %get-tuple-element.50) | copy-start | bytes 393220
  124.9 190.5 %copy-start.8 = (f32[1,2,128,128]{3,2,1,0:T(8,128)}, f32[1,2,128,128]{3,2,1,0:T(8,128)S(1)}, u32[]{:S(2)}) copy-start(f32[1,2,128,128]{3,2,1,0:T(8,128)S(1)} %get-tuple-element.51) | copy-start | bytes 393220
  333.0 109.2 %all-to-all-start.2 = ((f32[1,2,2,128,1024]{4,1,2,0,3:T(2,128)}), f32[1,2,2,128,1024]{4,1,2,0,3:T(2,128)}, u32[]{:S(2)}, u32[]{:S(2)}) async-start(f32[1,2,2,128,1024]{4,1,2,0,3:T(2,128)} %copy.78), calls=%async_computation.2 | async-start | bytes 4194304 | tf_op jit(solution)/shard_map/all_to_all | solution.py:70
  343.8 107.1 %copy-start.12 = (f32[1,64,128]{2,1,0:T(8,128)}, f32[1,64,128]{2,1,0:T(8,128)S(1)}, u32[]{:S(2)}) copy-start(f32[1,64,128]{2,1,0:T(8,128)S(1)} %get-tuple-element.68) | copy-start | bytes 98308
  450.9 11.9 copy-start.5
  455.2 41.6 %all-to-all-start.3 = ((f32[1,64,2,1024]{3,2,0,1:T(2,128)}), f32[1,64,2,1024]{3,2,0,1:T(2,128)S(1)}, u32[]{:S(2)}, u32[]{:S(2)}) async-start(f32[1,64,2,1024]{3,2,0,1:T(2,128)} %copy.81), calls=%async_computation.3 | async-start | bytes 1048576 | tf_op jit(solution)/shard_map/all_to_all | solution.py:78
  899.6 6.0 copy-start.13
  912.0 62.2 %all-to-all-start.7 = ((f32[2,64,2,1024]{3,2,0,1:T(2,128)}), f32[2,64,2,1024]{3,2,0,1:T(2,128)}, u32[]{:S(2)}, u32[]{:S(2)}) async-start(f32[2,64,2,1024]{3,2,0,1:T(2,128)} %copy.97), calls=%async_computation.7 | async-start | bytes 2097152 | tf_op jit(solution)/shard_map/all_to_all | solution.py:78
  920.2 99.0 %all-reduce.3.cloned.1.call-start = ((), (), s32[]{:S(2)}) async-start(), calls=%async_computation.8 | async-start | bytes 1048576 | tf_op jit(solution)/shard_map/psum | solution.py:150
  921.8 56.4 %copy-start.27 = (f32[1024]{0:T(1024)S(1)}, f32[1024]{0:T(1024)}, u32[]{:S(2)}) copy-start(f32[1024]{0:T(1024)} %param.12) | copy-start | bytes 12292
  921.8 56.4 %copy-start.28 = (f32[128]{0:T(128)S(1)}, f32[128]{0:T(128)}, u32[]{:S(2)}) copy-start(f32[128]{0:T(128)} %get-tuple-element.22) | copy-start | bytes 1540
  921.8 56.4 %copy-start.29 = (f32[128]{0:T(128)S(1)}, f32[128]{0:T(128)}, u32[]{:S(2)}) copy-start(f32[128]{0:T(128)} %get-tuple-element.57) | copy-start | bytes 1540
  921.8 56.4 %copy-start.30 = (f32[128]{0:T(128)S(1)}, f32[128]{0:T(128)}, u32[]{:S(2)}) copy-start(f32[128]{0:T(128)} %get-tuple-element.58) | copy-start | bytes 1540
  976.6 239.6 %all-gather.3.cloned.1.call-start = ((), (), s32[]{:S(2)}) async-start(), calls=%async_computation.9 | async-start | bytes 12681216 | tf_op jit(solution)/shard_map/all_gather | solution.py:151
  990.4 8.0 copy-start.6
  991.3 11.7 copy-start.4
  993.9 9.1 collective-permute-start.1
  (16 other events, 69.8 us)
Sparse Core Ops, SparseCore 0:
  976.7 42.4 all-reduce.2
Sparse Core Ops, SparseCore 1:
  991.4 224.7 all-gather.2
